TPU v7x, 256 devices: a whole 4x4x8 slice. The times are simulated.
256 devices in a mesh: term: 8 (over z), sec: 32 (over y, x, core).
Axes of the slice: x: 4, y: 4, z: 8, core: 2. Of those that a mesh axis runs over, the one named last changes fastest.
Arguments:
- start_vectors: bfloat16 [2, 64, 256, 256], P(None, 'sec'), may hold values from -6 to 6
- left_env: bfloat16 [32, 64, 256, 256], P('term', 'sec'), may hold values from -0.375 to 0.375
- right_env: bfloat16 [32, 64, 256, 256], P('term', 'sec'), may hold values from -0.375 to 0.375
- term_shift: int32 [32], P('term'), may hold values from -1 to 1
- precond: float32 [64, 256, 256], P('sec'), may hold values from 0.25 to 4
- block_dims: int32 [64], P('sec'), may hold values from 1 to 256, 8192 in all
Outputs:
- vector: float32 [2, 64, 256, 256], P(None, 'sec', 'term')
- energy: float32 [2], replicated
Inputs may be any that keep to these rules, and one draw needn't show every extreme that they name: `block_dims`: one block has exactly 256 live states.
All inputs are finite; a program needn't handle non-finite values.
Results may differ from a plain program's by a relative error of at most 0.0036.
Values may be sent and summed in bfloat16 or wider, within the bound.
No kernel may reach another device: no remote copies, remote signals or barrier semaphores. Data moves between devices by JAX's collectives and lax.ppermute only.
A program may use at most 64 MiB of HBM per device.

v0:
```python
import jax
import jax.numpy as jnp
from jax import lax
from jax.sharding import PartitionSpec as P

ITERS = 2


def padded(x, sides, width):
    for axis, dim in sides:
        count, length = (lax.axis_size(axis), x.shape[dim])
        up = [(i, (i + 1) % count) for i in range(count - 1)]
        down = [(j, i) for i, j in up]
        last = lax.slice_in_dim(x, length - width, length, axis=dim)
        initial = lax.slice_in_dim(x, 0, width, axis=dim)
        before = lax.ppermute(last, axis, up)
        after = lax.ppermute(initial, axis, down)
        x = jnp.concatenate([before, x, after], axis=dim)
    return x


def shards(start_vectors, left_env, right_env, term_shift, precond, block_dims):
    vec_count, blocks, states, _ = start_vectors.shape
    groups = lax.axis_size("term")
    share = states // groups
    offset_row = lax.axis_index("term") * share
    factor = 1.0 / (blocks * lax.axis_size("sec") * states * states)
    position = jnp.arange(states, dtype=jnp.int32)
    live_rows = position[None, :, None] < block_dims[:, None, None]
    live_cols = position[None, None, :] < block_dims[:, None, None]
    mask = (live_rows & live_cols).astype(jnp.float32)
    shift_sel = term_shift[:, None, None, None, None]

    def apply_op(vector_bf):
        local = jnp.einsum(
            "ujab,kjcb->kujac", vector_bf, right_env, preferred_element_type=jnp.float32
        ).astype(jnp.bfloat16)
        wide = padded(local, (("sec", 2),), 1)
        chosen = jnp.where(
            shift_sel < 0,
            wide[:, :, 0:blocks],
            jnp.where(shift_sel == 0, wide[:, :, 1 : blocks + 1], wide[:, :, 2 : blocks + 2]),
        )
        partial_sum = (
            jnp.einsum("kbac,kubcd->ubad", left_env, chosen, preferred_element_type=jnp.float32)
            * mask
        )
        result = lax.psum(partial_sum, "term")
        return result

    def totals(values):
        result = lax.psum(values, "sec")
        return result

    def inner(left, right):
        return jnp.sum(left * right, axis=(1, 2, 3)) * factor

    def expand(value):
        return value[:, None, None, None]

    start = start_vectors * mask.astype(jnp.bfloat16)
    h_vec = apply_op(start)
    vector = start.astype(jnp.float32)
    pre_view = precond[None]
    length = jnp.sqrt(totals(inner(vector, vector)[None])[0] + 1e-06)
    vector = vector / expand(length)
    h_vec = h_vec / expand(length)
    energy = jnp.zeros((vec_count,), jnp.float32)
    for iteration in range(ITERS):
        rayleigh = totals(inner(vector, h_vec)[None])[0]
        resid = h_vec - expand(rayleigh) * vector
        precon_res = pre_view * resid
        correlation = totals(inner(vector, precon_res)[None])[0]
        direction = precon_res - expand(correlation) * vector
        pair = totals(jnp.stack([inner(direction, direction), inner(direction, h_vec)]))
        square, raw_coupling = (pair[0], pair[1])
        dir_norm = jnp.sqrt(square + 1e-06)
        coupling = raw_coupling / dir_norm
        direction = direction / expand(dir_norm)
        widen_result = direction.astype(jnp.bfloat16)
        h_dir = apply_op(widen_result)
        curvature = totals(inner(direction, h_dir)[None])[0]
        energy = 0.5 * (rayleigh + curvature) - jnp.sqrt(
            (0.5 * (rayleigh - curvature)) ** 2 + coupling**2
        )
        weight = energy - rayleigh
        new_size = jnp.sqrt(coupling**2 + weight**2)
        vector = (expand(coupling) * vector + expand(weight) * direction) / expand(new_size)
        h_vec = (expand(coupling) * h_vec + expand(weight) * h_dir) / expand(new_size)
    final = lax.dynamic_slice_in_dim(vector, offset_row, share, 2)
    return (final, energy)


def solution(mesh):
    return jax.shard_map(
        shards,
        mesh=mesh,
        in_specs=(
            P(None, "sec", None, None),
            P("term", "sec", None, None),
            P("term", "sec", None, None),
            P("term"),
            P("sec", None, None),
            P("sec"),
        ),
        out_specs=(P(None, "sec", "term", None), P()),
        check_vma=False,
    )
```

profile of v0, /device:TPU:1, one launch (start us, length us, event | category | flops | bytes accessed | tf_op | source)
XLA Modules:
  0.0 827.7 jit_solution(5210906045877564215)
XLA Ops:
  10.7 4.6 collective-permute-start
  15.3 2.0 collective-permute-start.1
  17.3 9.7 %collective-permute-done = bf16[4,2,1,256,256]{4,3,0,1,2:T(8,128)(2,1)S(1)} collective-permute-done((bf16[4,2,1,256,256]{4,3,0,1,2:T(8,128)(2,1)S(1)}, bf16[4,2,1,256,256]{4,3,0,1,2:T(8,128)(2,1)S(1)}, u32[]{:S(2)}, u32[]{:S(2)}) %collective-permute-start) | collective-permute-done | bytes 1048608 | tf_op jit(solution)/shard_map/ppermute | solution.py:16
  27.1 4.4 collective-permute-done.1
  31.5 2.4 fusion.27
  34.3 61.0 %psum.85 = f32[1,2]{1,0:T(1,128)S(1)} all-reduce(f32[1,2]{1,0:T(1,128)S(1)} %multiply_bitcast_fusion.6), channel_id=1, replica_groups=mesh['term'=8,'sec'=32] {'sec'}, use_global_device_ids=true, to_apply=%region_2.3 | all-reduce | flops 2 | bytes 16 | tf_op jit(solution)/shard_map/psum | solution.py:52
  95.3 14.4 %all-reduce.4.cloned.1.call-done = f32[2,2,256,256]{2,3,0,1:T(8,128)} async-done(((f32[2,2,256,256]{2,3,0,1:T(8,128)}), f32[2,2,256,256]{2,3,0,1:T(8,128)}) %all-reduce.4.cloned.1.call-update) | async-done | bytes 1048592 | tf_op jit(solution)/shard_map/psum | solution.py:48
  112.6 67.1 %psum.86 = f32[2]{0:T(128)S(1)} all-reduce(f32[2]{0:T(128)S(1)} %broadcast_multiply_fusion.5), channel_id=1, replica_groups=mesh['term'=8,'sec'=32] {'sec'}, use_global_device_ids=true, to_apply=%region_4.5 | all-reduce | flops 2 | bytes 16 | tf_op jit(solution)/shard_map/psum | solution.py:52
  180.2 62.7 %psum.87 = f32[2]{0:T(128)S(1)} all-reduce(f32[2]{0:T(128)S(1)} %broadcast_multiply_fusion.4), channel_id=1, replica_groups=mesh['term'=8,'sec'=32] {'sec'}, use_global_device_ids=true, to_apply=%region_6.7 | all-reduce | flops 2 | bytes 16 | tf_op jit(solution)/shard_map/psum | solution.py:52
  244.5 62.7 %psum.88 = f32[2,2]{1,0:T(2,128)S(1)} all-reduce(f32[2,2]{1,0:T(2,128)S(1)} %pad_maximum_fusion.9), channel_id=1, replica_groups=mesh['term'=8,'sec'=32] {'sec'}, use_global_device_ids=true, to_apply=%region_9.10 | all-reduce | flops 4 | bytes 32 | tf_op jit(solution)/shard_map/psum | solution.py:52
  307.2 2.1 convert_bitcast_fusion.1
  309.5 2.1 collective-permute-start.2
  311.6 2.5 collective-permute-start.3
  314.0 9.2 %collective-permute-done.2 = bf16[4,2,1,256,256]{4,3,0,1,2:T(8,128)(2,1)S(1)} collective-permute-done((bf16[4,2,1,256,256]{4,3,0,1,2:T(8,128)(2,1)S(1)}, bf16[4,2,1,256,256]{4,3,0,1,2:T(8,128)(2,1)S(1)}, u32[]{:S(2)}, u32[]{:S(2)}) %collective-permute-start.2) | collective-permute-done | bytes 1048608 | tf_op jit(solution)/shard_map/ppermute | solution.py:16
  323.3 4.4 collective-permute-done.3
  327.7 2.4 fusion.33
  330.1 65.6 %all-reduce.6.cloned.1.call-done = f32[2,2,256,256]{2,3,0,1:T(8,128)} async-done(((f32[2,2,256,256]{2,3,0,1:T(8,128)}), f32[2,2,256,256]{2,3,0,1:T(8,128)}) %all-reduce.6.cloned.1.call-update) | async-done | bytes 1048592 | tf_op jit(solution)/shard_map/psum | solution.py:48
  397.7 67.1 %psum.90 = f32[2]{0:T(128)S(1)} all-reduce(f32[2]{0:T(128)S(1)} %broadcast_multiply_fusion.3), channel_id=1, replica_groups=mesh['term'=8,'sec'=32] {'sec'}, use_global_device_ids=true, to_apply=%region_12.13 | all-reduce | flops 2 | bytes 16 | tf_op jit(solution)/shard_map/psum | solution.py:52
  464.8 3.5 multiply_reduce_fusion.4
  468.3 62.8 %psum.91 = f32[2]{0:T(128)S(1)} all-reduce(f32[2]{0:T(128)S(1)} %broadcast_multiply_fusion.2), channel_id=1, replica_groups=mesh['term'=8,'sec'=32] {'sec'}, use_global_device_ids=true, to_apply=%region_14.15 | all-reduce | flops 2 | bytes 16 | tf_op jit(solution)/shard_map/psum | solution.py:52
  531.1 1.9 multiply_reduce_fusion.3
  533.0 62.7 %psum.92 = f32[2]{0:T(128)S(1)} all-reduce(f32[2]{0:T(128)S(1)} %broadcast_multiply_fusion.1), channel_id=1, replica_groups=mesh['term'=8,'sec'=32] {'sec'}, use_global_device_ids=true, to_apply=%region_16.17 | all-reduce | flops 2 | bytes 16 | tf_op jit(solution)/shard_map/psum | solution.py:52
  595.6 2.6 multiply_reduce_fusion.2
  598.2 62.7 %psum.93 = f32[2,2]{1,0:T(2,128)S(1)} all-reduce(f32[2,2]{1,0:T(2,128)S(1)} %pad_maximum_fusion.10), channel_id=1, replica_groups=mesh['term'=8,'sec'=32] {'sec'}, use_global_device_ids=true, to_apply=%region_19.20 | all-reduce | flops 4 | bytes 32 | tf_op jit(solution)/shard_map/psum | solution.py:52
  663.5 2.1 collective-permute-start.4
  665.6 2.5 collective-permute-start.5
  668.1 9.2 %collective-permute-done.4 = bf16[4,2,1,256,256]{4,3,0,1,2:T(8,128)(2,1)S(1)} collective-permute-done((bf16[4,2,1,256,256]{4,3,0,1,2:T(8,128)(2,1)S(1)}, bf16[4,2,1,256,256]{4,3,0,1,2:T(8,128)(2,1)S(1)}, u32[]{:S(2)}, u32[]{:S(2)}) %collective-permute-start.4) | collective-permute-done | bytes 1048608 | tf_op jit(solution)/shard_map/ppermute | solution.py:16
  677.3 4.4 collective-permute-done.5
  681.7 2.4 fusion.39
  684.1 65.3 %all-reduce.8.cloned.1.call-done = f32[2,2,256,256]{2,3,0,1:T(8,128)} async-done(((f32[2,2,256,256]{2,3,0,1:T(8,128)}), f32[2,2,256,256]{2,3,0,1:T(8,128)}) %all-reduce.8.cloned.1.call-update) | async-done | bytes 1048592 | tf_op jit(solution)/shard_map/psum | solution.py:48
  749.4 1.9 multiply_reduce_fusion
  751.3 67.1 %psum.95 = f32[2]{0:T(128)S(1)} all-reduce(f32[2]{0:T(128)S(1)} %broadcast_multiply_fusion), channel_id=1, replica_groups=mesh['term'=8,'sec'=32] {'sec'}, use_global_device_ids=true, to_apply=%region_22.23 | all-reduce | flops 2 | bytes 16 | tf_op jit(solution)/shard_map/psum | solution.py:52
  (63 shorter events, 16.4 us)
Async XLA Ops:
  7.2 2.5 copy-start
  7.2 102.5 %all-reduce.4.cloned.1.call-start = ((), (), s32[]{:S(2)}) async-start(), calls=%async_computation | async-start | bytes 2097152 | tf_op jit(solution)/shard_map/psum | solution.py:48
  8.2 23.3 %copy-start.4 = (f32[2,256,256]{1,2,0:T(8,128)}, f32[2,256,256]{1,2,0:T(8,128)S(1)}, u32[]{:S(2)}) copy-start(f32[2,256,256]{1,2,0:T(8,128)S(1)} %get-tuple-element.26) | copy-start | bytes 1572868
  10.5 6.8 copy-start.10
  10.5 21.0 %copy-start.7 = (bf16[4,2,256,256]{3,2,1,0:T(8,128)(2,1)S(1)}, bf16[4,2,256,256]{3,2,1,0:T(8,128)(2,1)}, u32[]{:S(2)}) copy-start(bf16[4,2,256,256]{3,2,1,0:T(8,128)(2,1)} %param.7) | copy-start | bytes 3145732
  10.7 16.4 %collective-permute-start = (bf16[4,2,1,256,256]{4,3,0,1,2:T(8,128)(2,1)S(1)}, bf16[4,2,1,256,256]{4,3,0,1,2:T(8,128)(2,1)S(1)}, u32[]{:S(2)}, u32[]{:S(2)}) collective-permute-start(bf16[4,2,1,256,256]{4,3,0,1,2:T(8,128)(2,1)S(1)} %get-tuple-element.24), channel_id=1, source_target_pairs={{0,1},{1,2},{2,3},{3,4},{4,5},{5,6},{6,7},{7,8},{8,9},{9,10},{10,1... | collective-permute-start | bytes 3145736 | tf_op jit(solution)/shard_map/ppermute | solution.py:16
  15.3 16.1 %collective-permute-start.1 = (bf16[4,2,1,256,256]{4,3,0,1,2:T(8,128)(2,1)S(1)}, bf16[4,2,1,256,256]{4,3,0,1,2:T(8,128)(2,1)S(1)}, u32[]{:S(2)}, u32[]{:S(2)}) collective-permute-start(bf16[4,2,1,256,256]{4,3,0,1,2:T(8,128)(2,1)S(1)} %get-tuple-element.25), channel_id=1, source_target_pairs={{1,0},{2,1},{3,2},{4,3},{5,4},{6,5},{7,6},{8,7},{9,8},{10,9},{11,1... | collective-permute-start | bytes 3145736 | tf_op jit(solution)/shard_map/ppermute | solution.py:17
  33.9 361.9 %all-reduce.6.cloned.1.call-start = ((), (), s32[]{:S(2)}) async-start(), calls=%async_computation.1 | async-start | bytes 2097152 | tf_op jit(solution)/shard_map/psum | solution.py:48
  109.7 70.1 %copy-start.1 = (f32[2,2,256,256]{2,3,0,1:T(8,128)S(1)}, f32[2,2,256,256]{2,3,0,1:T(8,128)}, u32[]{:S(2)}) copy-start(f32[2,2,256,256]{2,3,0,1:T(8,128)} %all-reduce.4.cloned.1.call-done) | copy-start | bytes 3145732
  309.3 18.4 %copy-start.5 = (f32[2,256,256]{1,2,0:T(8,128)S(1)}, f32[2,256,256]{1,2,0:T(8,128)}, u32[]{:S(2)}) copy-start(f32[2,256,256]{1,2,0:T(8,128)} %copy-done.4) | copy-start | bytes 1572868
  309.3 18.4 %copy-start.8 = (bf16[4,2,256,256]{3,2,1,0:T(8,128)(2,1)S(1)}, bf16[4,2,256,256]{3,2,1,0:T(8,128)(2,1)}, u32[]{:S(2)}) copy-start(bf16[4,2,256,256]{3,2,1,0:T(8,128)(2,1)} %param.7) | copy-start | bytes 3145732
  309.5 13.8 %collective-permute-start.2 = (bf16[4,2,1,256,256]{4,3,0,1,2:T(8,128)(2,1)S(1)}, bf16[4,2,1,256,256]{4,3,0,1,2:T(8,128)(2,1)S(1)}, u32[]{:S(2)}, u32[]{:S(2)}) collective-permute-start(bf16[4,2,1,256,256]{4,3,0,1,2:T(8,128)(2,1)S(1)} %get-tuple-element.22), channel_id=1, source_target_pairs={{0,1},{1,2},{2,3},{3,4},{4,5},{5,6},{6,7},{7,8},{8,9},{9,10},{10,1... | collective-permute-start | bytes 3145736 | tf_op jit(solution)/shard_map/ppermute | solution.py:16
  311.6 16.1 %collective-permute-start.3 = (bf16[4,2,1,256,256]{4,3,0,1,2:T(8,128)(2,1)S(1)}, bf16[4,2,1,256,256]{4,3,0,1,2:T(8,128)(2,1)S(1)}, u32[]{:S(2)}, u32[]{:S(2)}) collective-permute-start(bf16[4,2,1,256,256]{4,3,0,1,2:T(8,128)(2,1)S(1)} %get-tuple-element.23), channel_id=1, source_target_pairs={{1,0},{2,1},{3,2},{4,3},{5,4},{6,5},{7,6},{8,7},{9,8},{10,9},{11,1... | collective-permute-start | bytes 3145736 | tf_op jit(solution)/shard_map/ppermute | solution.py:17
  330.1 419.3 %all-reduce.8.cloned.1.call-start = ((), (), s32[]{:S(2)}) async-start(), calls=%async_computation.2 | async-start | bytes 2097152 | tf_op jit(solution)/shard_map/psum | solution.py:48
  468.3 127.4 %copy-start.2 = (f32[2,2,256,256]{2,3,0,1:T(8,128)S(1)}, f32[2,2,256,256]{2,3,0,1:T(8,128)}, u32[]{:S(2)}) copy-start(f32[2,2,256,256]{2,3,0,1:T(8,128)} %get-tuple-element.15) | copy-start | bytes 3145732
  662.3 1.0 copy-start.3
  663.4 18.4 %copy-start.6 = (f32[2,256,256]{1,2,0:T(8,128)S(1)}, f32[2,256,256]{1,2,0:T(8,128)}, u32[]{:S(2)}) copy-start(f32[2,256,256]{1,2,0:T(8,128)} %copy-done.4) | copy-start | bytes 1572868
  663.4 18.4 %copy-start.9 = (bf16[4,2,256,256]{3,2,1,0:T(8,128)(2,1)S(1)}, bf16[4,2,256,256]{3,2,1,0:T(8,128)(2,1)}, u32[]{:S(2)}) copy-start(bf16[4,2,256,256]{3,2,1,0:T(8,128)(2,1)} %param.7) | copy-start | bytes 3145732
  663.5 13.8 %collective-permute-start.4 = (bf16[4,2,1,256,256]{4,3,0,1,2:T(8,128)(2,1)S(1)}, bf16[4,2,1,256,256]{4,3,0,1,2:T(8,128)(2,1)S(1)}, u32[]{:S(2)}, u32[]{:S(2)}) collective-permute-start(bf16[4,2,1,256,256]{4,3,0,1,2:T(8,128)(2,1)S(1)} %get-tuple-element.20), channel_id=1, source_target_pairs={{0,1},{1,2},{2,3},{3,4},{4,5},{5,6},{6,7},{7,8},{8,9},{9,10},{10,1... | collective-permute-start | bytes 3145736 | tf_op jit(solution)/shard_map/ppermute | solution.py:16
  665.6 16.1 %collective-permute-start.5 = (bf16[4,2,1,256,256]{4,3,0,1,2:T(8,128)(2,1)S(1)}, bf16[4,2,1,256,256]{4,3,0,1,2:T(8,128)(2,1)S(1)}, u32[]{:S(2)}, u32[]{:S(2)}) collective-permute-start(bf16[4,2,1,256,256]{4,3,0,1,2:T(8,128)(2,1)S(1)} %get-tuple-element.21), channel_id=1, source_target_pairs={{1,0},{2,1},{3,2},{4,3},{5,4},{6,5},{7,6},{8,7},{9,8},{10,9},{11,1... | collective-permute-start | bytes 3145736 | tf_op jit(solution)/shard_map/ppermute | solution.py:17
Sparse Core Ops, SparseCore 0:
  34.0 75.5 all-reduce.3
  330.2 65.5 all-reduce.5
  684.2 65.1 all-reduce.7
where the time goes:
time: 829 us; the launch traced here: 828 us
  blocking collectives  576 us (69%)
  waiting for transfers between devices  187 us (23%)
  other arithmetic  20.1 us (2%)
  starting transfers between devices  15.8 us (2%)
  between operations  14 us (2%)
  matrix products  11 us (1%)
    psum x9, blocking collectives, totals(): result = lax.psum(values, 'sec')  576 us
    psum x3, waiting for transfers between devices, apply_op(): result = lax.psum(partial_sum, 'term')  145 us
    ppermute x3, waiting for transfers between devices, padded(): before = lax.ppermute(last, axis, up)  28.2 us
  transfers between devices with their start and end apart: 9, of which 9 were waited for; matrix products, arithmetic and copies ran while one was open for 0% of the time, Pallas kernels for 0%

commit v1 on v0

--- a/solution.py
+++ b/solution.py
@@ -45,7 +45,8 @@
             jnp.einsum("kbac,kubcd->ubad", left_env, chosen, preferred_element_type=jnp.float32)
             * mask
         )
-        result = lax.psum(partial_sum, "term")
+        parts = lax.all_gather(partial_sum, "term", axis=0, tiled=False)
+        result = parts.sum(axis=0)
         return result
 
     def totals(values):

time: 829 us -> 906 us (1.093)
  waiting for transfers between devices: 187 us -> 253 us
  other arithmetic: 20.1 us -> 33.1 us
    all_gather x0 -> x3, waiting for transfers between devices: none -> 212 us  [apply_op(): parts = lax.all_gather(partial_sum, 'term', axis=0, tiled=False)]
    psum x3 -> x0, waiting for transfers between devices: 145 us -> none  [apply_op(): result = lax.psum(partial_sum, 'term')]
    reduce_sum x0 -> x3, other arithmetic: none -> 14.1 us  [apply_op(): result = parts.sum(axis=0)]
where the time goes in v1:
time: 906 us; the launch traced here: 903 us
  blocking collectives  571 us (63%)
  waiting for transfers between devices  253 us (28%)
  other arithmetic  33.1 us (4%)
  starting transfers between devices  15.8 us (2%)
  between operations  14 us (2%)
  matrix products  11.1 us (1%)
    psum x9, blocking collectives, totals(): result = lax.psum(values, 'sec')  571 us
    all_gather x3, waiting for transfers between devices, apply_op(): parts = lax.all_gather(partial_sum, 'term', axis=0, tiled=False)  212 us
    ppermute x3, waiting for transfers between devices, padded(): before = lax.ppermute(last, axis, up)  28.2 us
  transfers between devices with their start and end apart: 9, of which 9 were waited for; matrix products, arithmetic and copies ran while one was open for 0% of the time, Pallas kernels for 0%

profile of v1, /device:TPU:1, one launch (start us, length us, event | category | flops | bytes accessed | tf_op | source)
XLA Modules:
  0.0 903.1 jit_solution(5213167288452984919)
XLA Ops:
  10.7 4.6 collective-permute-start
  17.3 9.7 %collective-permute-done = bf16[4,2,1,256,256]{4,3,0,1,2:T(8,128)(2,1)S(1)} collective-permute-done((bf16[4,2,1,256,256]{4,3,0,1,2:T(8,128)(2,1)S(1)}, bf16[4,2,1,256,256]{4,3,0,1,2:T(8,128)(2,1)S(1)}, u32[]{:S(2)}, u32[]{:S(2)}) %collective-permute-start) | collective-permute-done | bytes 1048608 | tf_op jit(solution)/shard_map/ppermute | solution.py:16
  27.1 4.4 collective-permute-done.1
  31.5 2.5 fusion.27
  34.3 61.0 %psum.63 = f32[1,2]{1,0:T(1,128)S(1)} all-reduce(f32[1,2]{1,0:T(1,128)S(1)} %multiply_bitcast_fusion.6), channel_id=1, replica_groups=mesh['term'=8,'sec'=32] {'sec'}, use_global_device_ids=true, to_apply=%region_2.3 | all-reduce | flops 2 | bytes 16 | tf_op jit(solution)/shard_map/psum | solution.py:53
  95.3 36.7 %all-gather.7.cloned.1.call-done = f32[16,2,256,256]{2,3,0,1:T(8,128)} async-done(((f32[2,2,256,256]{2,3,0,1:T(8,128)}), f32[16,2,256,256]{2,3,0,1:T(8,128)}) %all-gather.7.cloned.1.call-update) | async-done | bytes 8388624 | tf_op jit(solution)/shard_map/all_gather | solution.py:48
  132.0 4.1 reduce_sum.126
  137.7 62.9 %psum.64 = f32[2]{0:T(128)S(1)} all-reduce(f32[2]{0:T(128)S(1)} %broadcast_multiply_fusion.5), channel_id=1, replica_groups=mesh['term'=8,'sec'=32] {'sec'}, use_global_device_ids=true, to_apply=%region_4.5 | all-reduce | flops 2 | bytes 16 | tf_op jit(solution)/shard_map/psum | solution.py:53
  201.1 66.8 %psum.65 = f32[2]{0:T(128)S(1)} all-reduce(f32[2]{0:T(128)S(1)} %broadcast_multiply_fusion.4), channel_id=1, replica_groups=mesh['term'=8,'sec'=32] {'sec'}, use_global_device_ids=true, to_apply=%region_6.7 | all-reduce | flops 2 | bytes 16 | tf_op jit(solution)/shard_map/psum | solution.py:53
  269.5 62.7 %psum.66 = f32[2,2]{1,0:T(2,128)S(1)} all-reduce(f32[2,2]{1,0:T(2,128)S(1)} %pad_maximum_fusion.9), channel_id=1, replica_groups=mesh['term'=8,'sec'=32] {'sec'}, use_global_device_ids=true, to_apply=%region_9.10 | all-reduce | flops 4 | bytes 32 | tf_op jit(solution)/shard_map/psum | solution.py:53
  332.2 2.1 convert_bitcast_fusion.1
  334.6 2.1 collective-permute-start.2
  336.6 2.5 collective-permute-start.3
  339.1 9.2 %collective-permute-done.2 = bf16[4,2,1,256,256]{4,3,0,1,2:T(8,128)(2,1)S(1)} collective-permute-done((bf16[4,2,1,256,256]{4,3,0,1,2:T(8,128)(2,1)S(1)}, bf16[4,2,1,256,256]{4,3,0,1,2:T(8,128)(2,1)S(1)}, u32[]{:S(2)}, u32[]{:S(2)}) %collective-permute-start.2) | collective-permute-done | bytes 1048608 | tf_op jit(solution)/shard_map/ppermute | solution.py:16
  348.4 4.4 collective-permute-done.3
  352.8 2.4 fusion.33
  355.2 87.7 %all-gather.9.cloned.1.call-done = f32[16,2,256,256]{2,3,0,1:T(8,128)} async-done(((f32[2,2,256,256]{2,3,0,1:T(8,128)}), f32[16,2,256,256]{2,3,0,1:T(8,128)}) %all-gather.9.cloned.1.call-update) | async-done | bytes 8388624 | tf_op jit(solution)/shard_map/all_gather | solution.py:48
  442.9 5.0 reduce_sum.132
  449.8 62.9 %psum.67 = f32[2]{0:T(128)S(1)} all-reduce(f32[2]{0:T(128)S(1)} %broadcast_multiply_fusion.3), channel_id=1, replica_groups=mesh['term'=8,'sec'=32] {'sec'}, use_global_device_ids=true, to_apply=%region_12.13 | all-reduce | flops 2 | bytes 16 | tf_op jit(solution)/shard_map/psum | solution.py:53
  512.7 3.5 multiply_reduce_fusion.4
  516.1 66.9 %psum.68 = f32[2]{0:T(128)S(1)} all-reduce(f32[2]{0:T(128)S(1)} %broadcast_multiply_fusion.2), channel_id=1, replica_groups=mesh['term'=8,'sec'=32] {'sec'}, use_global_device_ids=true, to_apply=%region_14.15 | all-reduce | flops 2 | bytes 16 | tf_op jit(solution)/shard_map/psum | solution.py:53
  585.0 62.7 %psum.69 = f32[2]{0:T(128)S(1)} all-reduce(f32[2]{0:T(128)S(1)} %broadcast_multiply_fusion.1), channel_id=1, replica_groups=mesh['term'=8,'sec'=32] {'sec'}, use_global_device_ids=true, to_apply=%region_16.17 | all-reduce | flops 2 | bytes 16 | tf_op jit(solution)/shard_map/psum | solution.py:53
  647.6 2.6 multiply_reduce_fusion.2
  650.3 62.9 %psum.70 = f32[2,2]{1,0:T(2,128)S(1)} all-reduce(f32[2,2]{1,0:T(2,128)S(1)} %pad_maximum_fusion.10), channel_id=1, replica_groups=mesh['term'=8,'sec'=32] {'sec'}, use_global_device_ids=true, to_apply=%region_19.20 | all-reduce | flops 4 | bytes 32 | tf_op jit(solution)/shard_map/psum | solution.py:53
  715.7 2.1 collective-permute-start.4
  717.8 2.5 collective-permute-start.5
  720.3 9.2 %collective-permute-done.4 = bf16[4,2,1,256,256]{4,3,0,1,2:T(8,128)(2,1)S(1)} collective-permute-done((bf16[4,2,1,256,256]{4,3,0,1,2:T(8,128)(2,1)S(1)}, bf16[4,2,1,256,256]{4,3,0,1,2:T(8,128)(2,1)S(1)}, u32[]{:S(2)}, u32[]{:S(2)}) %collective-permute-start.4) | collective-permute-done | bytes 1048608 | tf_op jit(solution)/shard_map/ppermute | solution.py:16
  729.5 4.4 collective-permute-done.5
  733.9 2.4 fusion.39
  736.3 87.7 %all-gather.11.cloned.1.call-done = f32[16,2,256,256]{2,3,0,1:T(8,128)} async-done(((f32[2,2,256,256]{2,3,0,1:T(8,128)}), f32[16,2,256,256]{2,3,0,1:T(8,128)}) %all-gather.11.cloned.1.call-update) | async-done | bytes 8388624 | tf_op jit(solution)/shard_map/all_gather | solution.py:48
  824.0 5.0 reduce_sum.138
  830.9 62.9 %psum.71 = f32[2]{0:T(128)S(1)} all-reduce(f32[2]{0:T(128)S(1)} %broadcast_multiply_fusion), channel_id=1, replica_groups=mesh['term'=8,'sec'=32] {'sec'}, use_global_device_ids=true, to_apply=%region_22.23 | all-reduce | flops 2 | bytes 16 | tf_op jit(solution)/shard_map/psum | solution.py:53
  (64 shorter events, 20.9 us)
Async XLA Ops:
  7.2 2.5 copy-start
  7.2 124.8 %all-gather.7.cloned.1.call-start = ((), (), s32[]{:S(2)}) async-start(), calls=%async_computation | async-start | bytes 9437184 | tf_op jit(solution)/shard_map/all_gather | solution.py:48
  8.2 23.3 %copy-start.3 = (f32[2,256,256]{1,2,0:T(8,128)}, f32[2,256,256]{1,2,0:T(8,128)S(1)}, u32[]{:S(2)}) copy-start(f32[2,256,256]{1,2,0:T(8,128)S(1)} %get-tuple-element.26) | copy-start | bytes 1572868
  10.5 6.8 copy-start.9
  10.5 21.0 %copy-start.6 = (bf16[4,2,256,256]{3,2,1,0:T(8,128)(2,1)S(1)}, bf16[4,2,256,256]{3,2,1,0:T(8,128)(2,1)}, u32[]{:S(2)}) copy-start(bf16[4,2,256,256]{3,2,1,0:T(8,128)(2,1)} %param.7) | copy-start | bytes 3145732
  10.7 16.4 %collective-permute-start = (bf16[4,2,1,256,256]{4,3,0,1,2:T(8,128)(2,1)S(1)}, bf16[4,2,1,256,256]{4,3,0,1,2:T(8,128)(2,1)S(1)}, u32[]{:S(2)}, u32[]{:S(2)}) collective-permute-start(bf16[4,2,1,256,256]{4,3,0,1,2:T(8,128)(2,1)S(1)} %get-tuple-element.24), channel_id=1, source_target_pairs={{0,1},{1,2},{2,3},{3,4},{4,5},{5,6},{6,7},{7,8},{8,9},{9,10},{10,1... | collective-permute-start | bytes 3145736 | tf_op jit(solution)/shard_map/ppermute | solution.py:16
  15.3 16.1 %collective-permute-start.1 = (bf16[4,2,1,256,256]{4,3,0,1,2:T(8,128)(2,1)S(1)}, bf16[4,2,1,256,256]{4,3,0,1,2:T(8,128)(2,1)S(1)}, u32[]{:S(2)}, u32[]{:S(2)}) collective-permute-start(bf16[4,2,1,256,256]{4,3,0,1,2:T(8,128)(2,1)S(1)} %get-tuple-element.25), channel_id=1, source_target_pairs={{1,0},{2,1},{3,2},{4,3},{5,4},{6,5},{7,6},{8,7},{9,8},{10,9},{11,1... | collective-permute-start | bytes 3145736 | tf_op jit(solution)/shard_map/ppermute | solution.py:17
  33.9 408.9 %all-gather.9.cloned.1.call-start = ((), (), s32[]{:S(2)}) async-start(), calls=%async_computation.1 | async-start | bytes 9437184 | tf_op jit(solution)/shard_map/all_gather | solution.py:48
  334.4 18.4 %copy-start.4 = (f32[2,256,256]{1,2,0:T(8,128)S(1)}, f32[2,256,256]{1,2,0:T(8,128)}, u32[]{:S(2)}) copy-start(f32[2,256,256]{1,2,0:T(8,128)} %copy-done.3) | copy-start | bytes 1572868
  334.4 18.4 %copy-start.7 = (bf16[4,2,256,256]{3,2,1,0:T(8,128)(2,1)S(1)}, bf16[4,2,256,256]{3,2,1,0:T(8,128)(2,1)}, u32[]{:S(2)}) copy-start(bf16[4,2,256,256]{3,2,1,0:T(8,128)(2,1)} %param.7) | copy-start | bytes 3145732
  334.6 13.8 %collective-permute-start.2 = (bf16[4,2,1,256,256]{4,3,0,1,2:T(8,128)(2,1)S(1)}, bf16[4,2,1,256,256]{4,3,0,1,2:T(8,128)(2,1)S(1)}, u32[]{:S(2)}, u32[]{:S(2)}) collective-permute-start(bf16[4,2,1,256,256]{4,3,0,1,2:T(8,128)(2,1)S(1)} %get-tuple-element.22), channel_id=1, source_target_pairs={{0,1},{1,2},{2,3},{3,4},{4,5},{5,6},{6,7},{7,8},{8,9},{9,10},{10,1... | collective-permute-start | bytes 3145736 | tf_op jit(solution)/shard_map/ppermute | solution.py:16
  336.6 16.1 %collective-permute-start.3 = (bf16[4,2,1,256,256]{4,3,0,1,2:T(8,128)(2,1)S(1)}, bf16[4,2,1,256,256]{4,3,0,1,2:T(8,128)(2,1)S(1)}, u32[]{:S(2)}, u32[]{:S(2)}) collective-permute-start(bf16[4,2,1,256,256]{4,3,0,1,2:T(8,128)(2,1)S(1)} %get-tuple-element.23), channel_id=1, source_target_pairs={{1,0},{2,1},{3,2},{4,3},{5,4},{6,5},{7,6},{8,7},{9,8},{10,9},{11,1... | collective-permute-start | bytes 3145736 | tf_op jit(solution)/shard_map/ppermute | solution.py:17
  355.2 468.9 %all-gather.11.cloned.1.call-start = ((), (), s32[]{:S(2)}) async-start(), calls=%async_computation.2 | async-start | bytes 9437184 | tf_op jit(solution)/shard_map/all_gather | solution.py:48
  516.1 131.5 %copy-start.1 = (f32[2,2,256,256]{2,3,0,1:T(8,128)S(1)}, f32[2,2,256,256]{2,3,0,1:T(8,128)}, u32[]{:S(2)}) copy-start(f32[2,2,256,256]{2,3,0,1:T(8,128)} %get-tuple-element.15) | copy-start | bytes 3145732
  714.6 1.0 copy-start.2
  715.5 18.4 %copy-start.5 = (f32[2,256,256]{1,2,0:T(8,128)S(1)}, f32[2,256,256]{1,2,0:T(8,128)}, u32[]{:S(2)}) copy-start(f32[2,256,256]{1,2,0:T(8,128)} %copy-done.3) | copy-start | bytes 1572868
  715.5 18.4 %copy-start.8 = (bf16[4,2,256,256]{3,2,1,0:T(8,128)(2,1)S(1)}, bf16[4,2,256,256]{3,2,1,0:T(8,128)(2,1)}, u32[]{:S(2)}) copy-start(bf16[4,2,256,256]{3,2,1,0:T(8,128)(2,1)} %param.7) | copy-start | bytes 3145732
  715.7 13.8 %collective-permute-start.4 = (bf16[4,2,1,256,256]{4,3,0,1,2:T(8,128)(2,1)S(1)}, bf16[4,2,1,256,256]{4,3,0,1,2:T(8,128)(2,1)S(1)}, u32[]{:S(2)}, u32[]{:S(2)}) collective-permute-start(bf16[4,2,1,256,256]{4,3,0,1,2:T(8,128)(2,1)S(1)} %get-tuple-element.20), channel_id=1, source_target_pairs={{0,1},{1,2},{2,3},{3,4},{4,5},{5,6},{6,7},{7,8},{8,9},{9,10},{10,1... | collective-permute-start | bytes 3145736 | tf_op jit(solution)/shard_map/ppermute | solution.py:16
  717.8 16.1 %collective-permute-start.5 = (bf16[4,2,1,256,256]{4,3,0,1,2:T(8,128)(2,1)S(1)}, bf16[4,2,1,256,256]{4,3,0,1,2:T(8,128)(2,1)S(1)}, u32[]{:S(2)}, u32[]{:S(2)}) collective-permute-start(bf16[4,2,1,256,256]{4,3,0,1,2:T(8,128)(2,1)S(1)} %get-tuple-element.21), channel_id=1, source_target_pairs={{1,0},{2,1},{3,2},{4,3},{5,4},{6,5},{7,6},{8,7},{9,8},{10,9},{11,1... | collective-permute-start | bytes 3145736 | tf_op jit(solution)/shard_map/ppermute | solution.py:17
Sparse Core Ops, SparseCore 0:
  34.1 97.9 all-gather.6
  355.3 87.5 all-gather.8
  736.4 87.5 all-gather.10
